TPU v7x, 128 devices: a whole 4x4x4 slice. The times are simulated.
128 devices in a mesh: dp: 32 (over x, z, core), mp: 4 (over y).
Axes of the slice: x: 4, y: 4, z: 4, core: 2. Of those that a mesh axis runs over, the one named last changes fastest.
Arguments:
- hidden_in: bfloat16 [32768, 2048], P('dp', 'mp'), may hold values from -6 to 6
- token_ids: int32 [32768], P('dp'), may hold values from 0 to 128001, as said below
- passage_counts: int32 [64], P('dp'), may hold values from 1 to 4, as said below
- positive_doc: int32 [4096], P('dp'), may hold values from 0 to 63
- queries: bfloat16 [4096, 2048], P('dp', 'mp'), may hold values from -6 to 6
- norm_gain: float32 [2048], replicated, may hold values from 0.5 to 1.5
- w_gate: bfloat16 [2048, 7168], P(None, 'mp'), may hold values from -0.125 to 0.125
- w_up: bfloat16 [2048, 7168], P(None, 'mp'), may hold values from -0.125 to 0.125
- w_down: bfloat16 [7168, 2048], P('mp'), may hold values from -0.0625 to 0.0625
Outputs:
- query_loss: float32 [4096], P('dp')
- hidden_grad: bfloat16 [32768, 2048], P('dp', 'mp')
Inputs may be any that keep to these rules, and one draw needn't show every extreme that they name: `passage_counts`: A document has 1 to 4 passages; every draw has a dp index whose documents all have 4. The live passages hold 160 passages in all. `token_ids`: 128001 marks padding; it stands only at the tail of a document's last live passage, and every live passage has a token that is not padding.
All inputs are finite; a program needn't handle non-finite values.
Results may differ from a plain program's by a relative error of at most 0.023.
Values may be sent and summed in bfloat16 or wider, within the bound.
No kernel may reach another device: no remote copies, remote signals or barrier semaphores. Data moves between devices by JAX's collectives and lax.ppermute only.
A program may use at most 128 MiB of HBM per device.

v0:
```python
import math
import jax
import jax.numpy as jnp
from jax import lax
from jax.sharding import PartitionSpec as P

L = 128
pad_token = 128001
score_scale = 20.0
loss_seed = 4096.0
norm_epsilon = 1e-05
unit_epsilon = 1e-06


def sent_to_all(x, axis):
    copies = jnp.broadcast_to(x, (lax.axis_size(axis), *x.shape))
    return lax.all_to_all(copies, axis, split_axis=0, concat_axis=0, tiled=True)


def joined_along(blocks, dim):
    lengths = list(blocks.shape[1:])
    lengths[dim] *= blocks.shape[0]
    return jnp.moveaxis(blocks, 0, dim).reshape(lengths)


def gathered_copies(x, axis, dim):
    blocks = sent_to_all(x, axis)
    return joined_along(blocks, dim)


def cut_along(x, dim, devices):
    before, after = (x.shape[:dim], x.shape[dim + 1 :])
    return jnp.moveaxis(x.reshape(*before, devices, -1, *after), dim, 0)


def summed_on_arrival(x, axis, dim):
    blocks = cut_along(x, dim, lax.axis_size(axis))
    arrived = lax.all_to_all(blocks, axis, split_axis=0, concat_axis=0, tiled=True)
    return arrived.astype(jnp.float32).sum(axis=0)


def sent_together(arrays, axis, dim, along):
    widths = [math.prod(a.shape[along:]) for a in arrays]
    both = jnp.concatenate(
        [a.reshape(*a.shape[:along], w) for a, w in zip(arrays, widths)], axis=along
    )
    result = summed_on_arrival(both, axis, dim)
    blocks = jnp.split(result, [sum(widths[:k]) for k in range(1, len(widths))], axis=along)
    return tuple(
        (b.reshape(*result.shape[:along], *a.shape[along:]) for a, b in zip(arrays, blocks))
    )


def contract_rows(left, right):
    return lax.dot_general(
        left, right, (((1,), (1,)), ((), ())), preferred_element_type=jnp.float32
    )


def packing_order(received_flag, received_mask, slot_capacity):
    flag = received_flag.reshape(-1).astype(jnp.float32)
    place = jnp.cumsum(flag) - flag
    packed_rows = flag[None, :] * (
        place[None, :] == jnp.arange(slot_capacity, dtype=jnp.float32)[:, None]
    ).astype(jnp.float32)
    packed_half_rows = packed_rows.astype(jnp.bfloat16)
    task_row_mask = jnp.dot(
        packed_half_rows,
        received_mask.reshape(flag.shape[0], -1),
        preferred_element_type=jnp.float32,
    )
    return (packed_rows, packed_half_rows, task_row_mask)


def per_device(
    hidden_in, token_ids, passage_counts, positive_doc, queries, norm_gain, w_gate, w_up, w_down
):
    dp_count = lax.axis_size("dp")
    row_count, part_width = hidden_in.shape
    model_width = norm_gain.shape[0]
    docs_here = passage_counts.shape[0]
    quarters = 4
    block_len = L // quarters
    src_blocks = row_count // block_len
    most_pass = src_blocks // (docs_here * quarters)
    slot_count = src_blocks // dp_count
    slot_capacity = docs_here * 2 * (most_pass + 1)
    passes_here = docs_here * most_pass
    received = dp_count * slot_count
    all_counts = lax.all_gather(passage_counts, "dp", axis=0, tiled=True)
    doc_total = all_counts.shape[0]
    before = (jnp.arange(doc_total, dtype=jnp.int32) < lax.axis_index("dp") * docs_here).astype(
        jnp.int32
    )
    offset = quarters * jnp.sum(all_counts * before)
    block_index = jnp.arange(src_blocks, dtype=jnp.int32)
    live_block = block_index // quarters % most_pass < jnp.repeat(
        passage_counts, most_pass * quarters
    )
    live_int = live_block.astype(jnp.int32)
    global_order = offset + jnp.cumsum(live_int) - live_int
    target = global_order % dp_count
    token_live = (token_ids.reshape(src_blocks, block_len) != pad_token) & live_block[:, None]
    device_hit = live_block.astype(jnp.float32)[:, None] * (
        target[:, None] == jnp.arange(dp_count, dtype=jnp.int32)[None, :]
    ).astype(jnp.float32)
    earlier = jnp.cumsum(device_hit, axis=0) - device_hit
    slot_match = (
        earlier[:, :, None] == jnp.arange(slot_count, dtype=jnp.float32)[None, None, :]
    ).astype(jnp.float32)
    select = (device_hit[:, :, None] * slot_match).reshape(src_blocks, received).T
    select_half = select.astype(jnp.bfloat16)
    send_mask = jnp.dot(
        select_half, token_live.astype(jnp.bfloat16), preferred_element_type=jnp.float32
    )
    send_mask = send_mask.astype(jnp.bfloat16).reshape(dp_count, slot_count, block_len)
    send_flag = jnp.sum(select, axis=1).astype(jnp.bfloat16).reshape(dp_count, slot_count)
    mp_start = lax.axis_index("mp") * part_width
    send = jnp.dot(
        select_half,
        hidden_in.reshape(src_blocks, block_len * part_width),
        preferred_element_type=jnp.float32,
    )
    send = send.astype(jnp.bfloat16).reshape(dp_count, slot_count, block_len, part_width)
    got, received_mask, received_flag = (
        lax.all_to_all(send, "dp", split_axis=0, concat_axis=0, tiled=True),
        lax.all_to_all(send_mask, "dp", split_axis=0, concat_axis=0, tiled=True),
        lax.all_to_all(send_flag, "dp", split_axis=0, concat_axis=0, tiled=True),
    )
    packed_rows, packed_half_rows, task_row_mask = packing_order(
        received_flag, received_mask, slot_capacity
    )
    own_rows = jnp.dot(
        packed_half_rows,
        got.reshape(received, block_len * part_width),
        preferred_element_type=jnp.float32,
    )
    own_rows = own_rows.astype(jnp.bfloat16).reshape(slot_capacity * block_len, part_width)
    task_rows = gathered_copies(own_rows, "mp", 1)
    row_float = task_rows.astype(jnp.float32)
    rms_scale = lax.rsqrt(jnp.mean(row_float * row_float, axis=1, keepdims=True) + norm_epsilon)
    normed = (row_float * rms_scale * norm_gain[None, :]).astype(jnp.bfloat16)
    gate = jnp.dot(normed, w_gate, preferred_element_type=jnp.float32)
    up = jnp.dot(normed, w_up, preferred_element_type=jnp.float32)
    sigmoid_gate = jax.nn.sigmoid(gate)
    hidden = (gate * sigmoid_gate * up).astype(jnp.bfloat16)
    layer_part = jnp.dot(hidden, w_down, preferred_element_type=jnp.float32)
    token_weight = task_row_mask[:, :, None]
    layer_pool = jnp.sum(
        layer_part.reshape(slot_capacity, block_len, model_width) * token_weight, axis=1
    )
    layer_pool = summed_on_arrival(layer_pool.astype(jnp.bfloat16), "mp", 1)
    own_input = own_rows.astype(jnp.float32)
    pooled = (
        jnp.sum(own_input.reshape(slot_capacity, block_len, part_width) * token_weight, axis=1)
        + layer_pool
    )
    spread = jnp.dot(packed_rows.T, pooled)
    home = lax.all_to_all(
        spread.reshape(dp_count, slot_count, part_width).astype(jnp.bfloat16),
        "dp",
        split_axis=0,
        concat_axis=0,
        tiled=True,
    ).astype(jnp.float32)
    block_sums = jnp.dot(select.T, home.reshape(received, part_width))
    passage_sum = block_sums.reshape(passes_here, quarters, part_width).sum(axis=1)
    token_total = jnp.sum(
        token_live.reshape(passes_here, quarters * block_len).astype(jnp.float32), axis=1
    )
    divisor = jnp.maximum(token_total, 1.0)
    passage_vec = (passage_sum / divisor[:, None]).astype(jnp.bfloat16)
    all_vec = lax.all_gather(passage_vec, "dp", axis=0, tiled=True)
    pass_total = all_vec.shape[0]
    all_live = (
        jnp.arange(pass_total, dtype=jnp.int32) % most_pass < jnp.repeat(all_counts, most_pass)
    ).astype(jnp.float32)
    vec_float = all_vec.astype(jnp.float32)
    query_float = queries.astype(jnp.float32)
    score_part = contract_rows(queries, all_vec)
    raw_score, passage_sq, query_sq = (
        lax.psum(score_part.astype(jnp.bfloat16), "mp").astype(jnp.float32),
        lax.psum(jnp.sum(vec_float * vec_float, axis=1).astype(jnp.bfloat16), "mp").astype(
            jnp.float32
        ),
        lax.psum(jnp.sum(query_float * query_float, axis=1).astype(jnp.bfloat16), "mp").astype(
            jnp.float32
        ),
    )
    query_scale = lax.rsqrt(query_sq + unit_epsilon)
    passage_scale = lax.rsqrt(passage_sq + unit_epsilon)
    scores = score_scale * raw_score * query_scale[:, None] * passage_scale[None, :]
    weights = all_live[None, :] * jnp.exp(scores)
    doc_mass = weights.reshape(queries.shape[0], doc_total, most_pass).sum(axis=2)
    total_mass = doc_mass.sum(axis=1)
    positive_hit = (
        positive_doc[:, None] == jnp.arange(doc_total, dtype=jnp.int32)[None, :]
    ).astype(jnp.float32)
    positive_mass = jnp.sum(doc_mass * positive_hit, axis=1)
    query_loss = jnp.log(total_mass) - jnp.log(positive_mass)
    positive_pass = jnp.repeat(positive_hit, most_pass, axis=1)
    coefficient = (
        loss_seed
        * score_scale
        * query_scale[:, None]
        * (weights / total_mass[:, None] - positive_pass * weights / positive_mass[:, None])
    )
    weighted_queries = lax.dot_general(
        coefficient.astype(jnp.bfloat16),
        queries,
        (((0,), (0,)), ((), ())),
        preferred_element_type=jnp.float32,
    )
    norm_term = jnp.sum(coefficient * raw_score, axis=0)
    vec_grad, norm_grad = sent_together(
        (weighted_queries.astype(jnp.bfloat16), norm_term.astype(jnp.bfloat16)), "dp", 0, 1
    )
    own_scale = lax.dynamic_slice_in_dim(
        passage_scale, lax.axis_index("dp") * passes_here, passes_here
    )
    own_vec = passage_vec.astype(jnp.float32)
    vec_change = own_scale[:, None] * vec_grad - own_vec * (own_scale**3 * norm_grad)[:, None]
    token_grad = (vec_change / divisor[:, None]).astype(jnp.bfloat16)
    block_grad = jnp.repeat(token_grad, quarters, axis=0)
    grad_send = jnp.dot(select_half, block_grad, preferred_element_type=jnp.float32).astype(
        jnp.bfloat16
    )
    grad_got = lax.all_to_all(
        grad_send.reshape(dp_count, slot_count, part_width),
        "dp",
        split_axis=0,
        concat_axis=0,
        tiled=True,
    )
    grad_task = jnp.dot(
        packed_half_rows, grad_got.reshape(received, part_width), preferred_element_type=jnp.float32
    ).astype(jnp.bfloat16)
    grad_full = lax.all_gather(grad_task, "mp", axis=1, tiled=True)
    out_grad = (
        (token_weight * grad_full[:, None, :].astype(jnp.float32))
        .astype(jnp.bfloat16)
        .reshape(slot_capacity * block_len, model_width)
    )
    own_out_grad = (token_weight * grad_task[:, None, :].astype(jnp.float32)).reshape(
        slot_capacity * block_len, part_width
    )
    hidden_grad = contract_rows(out_grad, w_down)
    gate_grad = (hidden_grad * up * sigmoid_gate * (1.0 + gate * (1.0 - sigmoid_gate))).astype(
        jnp.bfloat16
    )
    up_grad = (hidden_grad * gate * sigmoid_gate).astype(jnp.bfloat16)
    normed_grad = contract_rows(gate_grad, w_gate) + contract_rows(up_grad, w_up)
    own_gain = lax.dynamic_slice_in_dim(norm_gain, mp_start, part_width)
    own_normed = lax.psum_scatter(
        normed_grad.astype(jnp.bfloat16), "mp", scatter_dimension=1, tiled=True
    ).astype(jnp.float32)
    inner_part = jnp.sum(own_input * own_gain[None, :] * own_normed, axis=1)
    inner = lax.psum(inner_part, "mp") / model_width
    input_grad = (
        own_out_grad
        + rms_scale * own_gain[None, :] * own_normed
        - own_input * rms_scale**3 * inner[:, None]
    )
    input_half = input_grad.astype(jnp.bfloat16).reshape(slot_capacity, block_len * part_width)
    back = jnp.dot(packed_half_rows.T, input_half, preferred_element_type=jnp.float32).astype(
        jnp.bfloat16
    )
    back_got = lax.all_to_all(
        back.reshape(dp_count, slot_count, block_len * part_width),
        "dp",
        split_axis=0,
        concat_axis=0,
        tiled=True,
    )
    grad_rows = jnp.dot(
        select_half.T,
        back_got.reshape(received, block_len * part_width),
        preferred_element_type=jnp.float32,
    )
    return (query_loss, grad_rows.astype(jnp.bfloat16).reshape(row_count, part_width))


def solution(mesh):
    return jax.shard_map(
        per_device,
        mesh=mesh,
        in_specs=(
            P("dp", "mp"),
            P("dp"),
            P("dp"),
            P("dp"),
            P("dp", "mp"),
            P(),
            P(None, "mp"),
            P(None, "mp"),
            P("mp", None),
        ),
        out_specs=(P("dp"), P("dp", "mp")),
        check_vma=False,
    )
```

profile of v0, /device:TPU:1, one launch (start us, length us, event | category | flops | bytes accessed | tf_op | source)
XLA Modules:
  0.0 400.2 jit_solution(1453509648983306713)
XLA Ops:
  11.0 15.5 %all-reduce = s32[64]{0:T(128)S(1)} all-reduce(s32[64]{0:T(128)S(1)} %dynamic-update-slice), channel_id=1, replica_groups=mesh['dp'=32,'mp'=4] {'dp'}, use_global_device_ids=true, to_apply=%add | all-reduce | flops 64 | bytes 512
  29.0 7.5 %all-to-all-start = ((bf16[32,1,1]{2,1,0:T(2,128)(2,1)}), bf16[32,1,1]{2,1,0:T(2,128)(2,1)S(1)}, u32[]{:S(2)}, u32[]{:S(2)}) async-start(bf16[32,1,1]{2,1,0:T(2,128)(2,1)} %copy.74), calls=%async_computation | async-start | bytes 32768 | tf_op jit(solution)/shard_map/all_to_all | solution.py:128
  49.2 15.6 %all-to-all-done.1 = bf16[32,1,32,512]{3,2,1,0:T(8,128)(2,1)S(1)} async-done(((bf16[32,1,32,512]{3,2,1,0:T(8,128)(2,1)}), bf16[32,1,32,512]{3,2,1,0:T(8,128)(2,1)S(1)}, u32[]{:S(2)}, u32[]{:S(2)}) %all-to-all-start.1) | async-done | bytes 1048608 | tf_op jit(solution)/shard_map/all_to_all | solution.py:126
  77.3 4.8 %all-to-all-start.3 = ((bf16[4,640,512]{1,2,0:T(8,128)(2,1)}), bf16[4,640,512]{1,2,0:T(8,128)(2,1)S(1)}, u32[]{:S(2)}, u32[]{:S(2)}) async-start(bf16[4,640,512]{1,2,0:T(8,128)(2,1)} %broadcast_in_dim.18), calls=%async_computation.3 | async-start | bytes 5242880 | tf_op jit(solution)/shard_map/all_to_all | solution.py:17
  86.4 26.3 %all-to-all-done.3 = bf16[4,640,512]{1,2,0:T(8,128)(2,1)S(1)} async-done(((bf16[4,640,512]{1,2,0:T(8,128)(2,1)}), bf16[4,640,512]{1,2,0:T(8,128)(2,1)S(1)}, u32[]{:S(2)}, u32[]{:S(2)}) %all-to-all-start.3) | async-done | bytes 2621472 | tf_op jit(solution)/shard_map/all_to_all | solution.py:17
  114.0 8.6 %fusion.85 = f32[640,1792]{1,0:T(8,128)S(1)} fusion(bf16[640,2048]{0,1:T(8,128)(2,1)S(1)} %fusion.2, bf16[2048,1792]{1,0:T(8,128)(2,1)} %param.16), kind=kOutput, calls=%fused_computation.172 | convolution fusion | flops 4697620480 | bytes 14548992 | tf_op jit(solution)/shard_map/dot_general | solution.py:144
  122.7 5.4 %fusion.84 = f32[640,1792]{1,0:T(8,128)S(1)} fusion(bf16[640,2048]{0,1:T(8,128)(2,1)S(1)} %fusion.2, bf16[2048,1792]{1,0:T(8,128)(2,1)S(1)} %bitcast.102), kind=kOutput, calls=%fused_computation.171 | convolution fusion | flops 4697620480 | bytes 14548992 | tf_op jit(solution)/shard_map/dot_general | solution.py:143
  128.2 5.0 %fusion.4 = f32[640,2048]{1,0:T(8,128)S(1)} fusion(bf16[1792,2048]{1,0:T(8,128)(2,1)S(1)} %bitcast.100, f32[640,1792]{1,0:T(8,128)S(1)} %fusion.85, f32[640,1792]{1,0:T(8,128)S(1)} %fusion.84), kind=kOutput, calls=%fused_computation.17 | convolution fusion | flops 4704501760 | bytes 21757952 | tf_op jit(solution)/shard_map/dot_general | solution.py:147
  144.8 6.5 %all-to-all-start.5 = ((bf16[32,2,256]{2,1,0:T(2,128)(2,1)}), bf16[32,2,256]{2,1,0:T(2,128)(2,1)S(1)}, u32[]{:S(2)}, u32[]{:S(2)}) async-start(bf16[32,2,256]{2,1,0:T(2,128)(2,1)} %reshape.475), calls=%async_computation.5 | async-start | bytes 65536 | tf_op jit(solution)/shard_map/all_to_all | solution.py:159
  151.6 7.1 %all-to-all-done.5 = bf16[32,2,256]{2,1,0:T(2,128)(2,1)S(1)} async-done(((bf16[32,2,256]{2,1,0:T(2,128)(2,1)}), bf16[32,2,256]{2,1,0:T(2,128)(2,1)S(1)}, u32[]{:S(2)}, u32[]{:S(2)}) %all-to-all-start.5) | async-done | bytes 32800 | tf_op jit(solution)/shard_map/all_to_all | solution.py:159
  159.0 23.1 %all_gather.10 = bf16[256,512]{1,0:T(8,128)(2,1)S(1)} all-gather(bf16[8,512]{1,0:T(8,128)(2,1)S(1)} %divide_convert_fusion), channel_id=1, replica_groups=mesh['dp'=32,'mp'=4] {'dp'}, dimensions={0}, use_global_device_ids=true | all-gather | bytes 270336 | tf_op jit(solution)/shard_map/all_gather | solution.py:173
  183.1 6.9 %all-reduce.1 = (bf16[256]{0:T(256)(128)(2,1)S(1)}, bf16[128]{0:T(256)(128)(2,1)S(1)}) all-reduce(bf16[256]{0:T(256)(128)(2,1)S(1)} %multiply_reduce_fusion.2, bf16[128]{0:T(256)(128)(2,1)S(1)} %multiply_reduce_fusion.3), channel_id=1, replica_groups=mesh['dp'=32,'mp'=4] {'mp'}, use_global_device_ids=true, to_apply=%region_15.16 | all-reduce | flops 384 | bytes 1536 | tf_op jit(solution)/shard_map/psum | solution.py:183
  190.0 37.0 %all-reduce.4.cloned.1.call-done = bf16[128,256]{0,1:T(8,128)(2,1)} async-done(((bf16[128,256]{0,1:T(8,128)(2,1)}), bf16[128,256]{0,1:T(8,128)(2,1)}) %all-reduce.4.cloned.1.call-update) | async-done | bytes 65552 | tf_op jit(solution)/shard_map/psum | solution.py:182
  231.3 9.7 %all-to-all-start.6 = ((bf16[32,8,513]{2,1,0:T(8,128)(2,1)}), bf16[32,8,513]{2,1,0:T(8,128)(2,1)S(1)}, u32[]{:S(2)}, u32[]{:S(2)}) async-start(bf16[32,8,513]{2,1,0:T(8,128)(2,1)} %pad_maximum_fusion), calls=%async_computation.6 | async-start | bytes 655360 | tf_op jit(solution)/shard_map/all_to_all | solution.py:38
  241.0 9.6 %all-to-all-done.6 = bf16[32,8,513]{2,1,0:T(8,128)(2,1)S(1)} async-done(((bf16[32,8,513]{2,1,0:T(8,128)(2,1)}), bf16[32,8,513]{2,1,0:T(8,128)(2,1)S(1)}, u32[]{:S(2)}, u32[]{:S(2)}) %all-to-all-start.6) | async-done | bytes 262688 | tf_op jit(solution)/shard_map/all_to_all | solution.py:38
  256.2 7.1 %all-to-all-done.7 = bf16[32,2,256]{2,1,0:T(2,128)(2,1)S(1)} async-done(((bf16[32,2,256]{2,1,0:T(2,128)(2,1)}), bf16[32,2,256]{2,1,0:T(2,128)(2,1)S(1)}, u32[]{:S(2)}, u32[]{:S(2)}) %all-to-all-start.7) | async-done | bytes 32800 | tf_op jit(solution)/shard_map/all_to_all | solution.py:228
  263.5 9.0 %all_gather.11 = bf16[20,2048]{1,0:T(8,128)(2,1)S(1)} all-gather(bf16[20,512]{1,0:T(8,128)(2,1)S(1)} %get-tuple-element.20), channel_id=1, replica_groups=mesh['dp'=32,'mp'=4] {'mp'}, dimensions={1}, use_global_device_ids=true | all-gather | bytes 102400 | tf_op jit(solution)/shard_map/all_gather | solution.py:238
  272.9 10.2 %fusion.86 = f32[640,1792]{1,0:T(8,128)} fusion(bf16[640,2048]{1,0:T(8,128)(2,1)S(1)} %fusion.3, bf16[1792,2048]{1,0:T(8,128)(2,1)} %param.17), kind=kOutput, calls=%fused_computation.173 | convolution fusion | flops 4697620480 | bytes 14548992 | tf_op jit(solution)/shard_map/dot_general | solution.py:55
  283.1 14.2 %fusion.7 = f32[640,2048]{1,0:T(8,128)} fusion(bf16[2048,1792]{1,0:T(8,128)(2,1)S(1)} %bitcast.104, f32[640,1792]{1,0:T(8,128)} %copy-done.6, f32[640,1792]{1,0:T(8,128)} %fusion.86, f32[640,1792]{1,0:T(8,128)} %copy-done.7), kind=kOutput, calls=%fused_computation.20 | convolution fusion | flops 4709089280 | bytes 26345472 | tf_op jit(solution)/shard_map/dot_general | solution.py:55
  297.4 13.7 %add_convert_fusion = bf16[640,2048]{1,0:T(8,128)(2,1)} fusion(f32[640,2048]{1,0:T(8,128)} %fusion.7, bf16[2048,1792]{1,0:T(8,128)(2,1)} %param.16, f32[640,1792]{1,0:T(8,128)} %fusion.86, f32[640,1792]{1,0:T(8,128)} %copy-done.6), kind=kOutput, calls=%fused_computation.10 | convolution fusion | flops 4707123200 | bytes 24379392 | tf_op jit(solution)/shard_map/dot_general | solution.py:55
  311.1 32.8 %reduce-scatter.2.cloned.1.call-done = bf16[640,512]{1,0:T(8,128)(2,1)} async-done(((bf16[640,2048]{1,0:T(8,128)(2,1)}), bf16[640,512]{1,0:T(8,128)(2,1)}) %reduce-scatter.2.cloned.1.call-update) | async-done | bytes 655376 | tf_op jit(solution)/shard_map/reduce_scatter | solution.py:254
  345.3 6.5 %psum.31 = f32[640]{0:T(1024)S(1)} all-reduce(f32[640]{0:T(1024)S(1)} %fusion.11), channel_id=1, replica_groups=mesh['dp'=32,'mp'=4] {'mp'}, use_global_device_ids=true, to_apply=%region_23.24 | all-reduce | flops 640 | bytes 5120 | tf_op jit(solution)/shard_map/psum | solution.py:258
  357.3 9.7 %all-to-all-start.8 = ((bf16[32,2,8192]{2,1,0:T(2,128)(2,1)}), bf16[32,2,8192]{2,1,0:T(2,128)(2,1)}, u32[]{:S(2)}, u32[]{:S(2)}) async-start(bf16[32,2,8192]{2,1,0:T(2,128)(2,1)} %reshape.479), calls=%async_computation.9 | async-start | bytes 2097152 | tf_op jit(solution)/shard_map/all_to_all | solution.py:268
  367.6 16.4 %all-to-all-done.8 = bf16[32,2,8192]{2,1,0:T(2,128)(2,1)} async-done(((bf16[32,2,8192]{2,1,0:T(2,128)(2,1)}), bf16[32,2,8192]{2,1,0:T(2,128)(2,1)}, u32[]{:S(2)}, u32[]{:S(2)}) %all-to-all-start.8) | async-done | bytes 1048608 | tf_op jit(solution)/shard_map/all_to_all | solution.py:268
  (145 shorter events, 75.9 us)
Async XLA Ops:
  7.2 40.6 %copy-start.3 = (s32[1024]{0:T(1024)S(1)}, s32[1024]{0:T(1024)}, u32[]{:S(2)}) copy-start(s32[1024]{0:T(1024)} %param.10) | copy-start | bytes 12292
  29.0 14.5 %all-to-all-start = ((bf16[32,1,1]{2,1,0:T(2,128)(2,1)}), bf16[32,1,1]{2,1,0:T(2,128)(2,1)S(1)}, u32[]{:S(2)}, u32[]{:S(2)}) async-start(bf16[32,1,1]{2,1,0:T(2,128)(2,1)} %copy.74), calls=%async_computation | async-start | bytes 32768 | tf_op jit(solution)/shard_map/all_to_all | solution.py:128
  43.5 21.2 %all-to-all-start.1 = ((bf16[32,1,32,512]{3,2,1,0:T(8,128)(2,1)}), bf16[32,1,32,512]{3,2,1,0:T(8,128)(2,1)S(1)}, u32[]{:S(2)}, u32[]{:S(2)}) async-start(bf16[32,1,32,512]{3,2,1,0:T(8,128)(2,1)} %bitcast.5), calls=%async_computation.1 | async-start | bytes 2097152 | tf_op jit(solution)/shard_map/all_to_all | solution.py:126
  64.7 10.9 %all-to-all-start.2 = ((bf16[32,1,32]{2,1,0:T(2,128)(2,1)}), bf16[32,1,32]{2,1,0:T(2,128)(2,1)S(1)}, u32[]{:S(2)}, u32[]{:S(2)}) async-start(bf16[32,1,32]{2,1,0:T(2,128)(2,1)} %copy.77), calls=%async_computation.2 | async-start | bytes 32768 | tf_op jit(solution)/shard_map/all_to_all | solution.py:127
  71.6 10.6 %copy-start.5 = (s32[2]{0:T(128)S(1)}, s32[2]{0:T(128)}, u32[]{:S(2)}) copy-start(s32[2]{0:T(128)} %param.11) | copy-start | bytes 28
  71.6 11.2 %copy-start.4 = (s32[128]{0:T(128)S(1)}, s32[128]{0:T(128)}, u32[]{:S(2)}) copy-start(s32[128]{0:T(128)} %param.12) | copy-start | bytes 1540
  77.3 36.0 %copy-start.2 = (f32[2048]{0:T(1024)S(1)}, f32[2048]{0:T(1024)}, u32[]{:S(2)}) copy-start(f32[2048]{0:T(1024)} %param.14) | copy-start | bytes 24580
  77.3 35.4 %all-to-all-start.3 = ((bf16[4,640,512]{1,2,0:T(8,128)(2,1)}), bf16[4,640,512]{1,2,0:T(8,128)(2,1)S(1)}, u32[]{:S(2)}, u32[]{:S(2)}) async-start(bf16[4,640,512]{1,2,0:T(8,128)(2,1)} %broadcast_in_dim.18), calls=%async_computation.3 | async-start | bytes 5242880 | tf_op jit(solution)/shard_map/all_to_all | solution.py:17
  113.3 9.3 %slice-start.2 = ((s8[7340032]{0:T(1024)(128)(4,1)}), s8[4194304]{0:T(1024)(128)(4,1)S(1)}, s32[]{:S(2)}) async-start(s8[7340032]{0:T(1024)(128)(4,1)} %bitcast.101), calls=%async_computation.14 | async-start | bytes 8388608
  113.3 14.8 %slice-start = ((s8[7340032]{0:T(1024)(128)(4,1)}), s8[4194304]{0:T(1024)(128)(4,1)S(1)}, s32[]{:S(2)}) async-start(s8[7340032]{0:T(1024)(128)(4,1)} %bitcast.99), calls=%async_computation.12 | async-start | bytes 8388608
  114.0 8.7 %slice-start.3 = ((s8[7340032]{0:T(1024)(128)(4,1)}), s8[3145728]{0:T(1024)(128)(4,1)S(1)}, s32[]{:S(2)}) async-start(s8[7340032]{0:T(1024)(128)(4,1)} %bitcast.101), calls=%async_computation.15 | async-start | bytes 6291456
  114.0 14.2 %slice-start.1 = ((s8[7340032]{0:T(1024)(128)(4,1)}), s8[3145728]{0:T(1024)(128)(4,1)S(1)}, s32[]{:S(2)}) async-start(s8[7340032]{0:T(1024)(128)(4,1)} %bitcast.99), calls=%async_computation.13 | async-start | bytes 6291456
  122.7 5.5 %copy-start.7 = (f32[640,1792]{1,0:T(8,128)}, f32[640,1792]{1,0:T(8,128)S(1)}, u32[]{:S(2)}) copy-start(f32[640,1792]{1,0:T(8,128)S(1)} %fusion.85) | copy-start | bytes 13762564
  128.2 5.0 %copy-start.6 = (f32[640,1792]{1,0:T(8,128)}, f32[640,1792]{1,0:T(8,128)S(1)}, u32[]{:S(2)}) copy-start(f32[640,1792]{1,0:T(8,128)S(1)} %fusion.84) | copy-start | bytes 13762564
  133.2 18.2 %copy-start.1 = (bf16[128,512]{1,0:T(8,128)(2,1)S(1)}, bf16[128,512]{1,0:T(8,128)(2,1)}, u32[]{:S(2)}) copy-start(bf16[128,512]{1,0:T(8,128)(2,1)} %param.13) | copy-start | bytes 393220
  134.9 7.9 %all-to-all-start.4 = ((bf16[4,20,512]{2,1,0:T(8,128)(2,1)}), bf16[4,20,512]{2,1,0:T(8,128)(2,1)S(1)}, u32[]{:S(2)}, u32[]{:S(2)}) async-start(bf16[4,20,512]{2,1,0:T(8,128)(2,1)} %copy.79), calls=%async_computation.4 | async-start | bytes 196608 | tf_op jit(solution)/shard_map/all_to_all | solution.py:38
  144.8 13.9 %all-to-all-start.5 = ((bf16[32,2,256]{2,1,0:T(2,128)(2,1)}), bf16[32,2,256]{2,1,0:T(2,128)(2,1)S(1)}, u32[]{:S(2)}, u32[]{:S(2)}) async-start(bf16[32,2,256]{2,1,0:T(2,128)(2,1)} %reshape.475), calls=%async_computation.5 | async-start | bytes 65536 | tf_op jit(solution)/shard_map/all_to_all | solution.py:159
  151.3 75.6 %all-reduce.4.cloned.1.call-start = ((), (), s32[]{:S(2)}) async-start(), calls=%async_computation.10 | async-start | bytes 131072 | tf_op jit(solution)/shard_map/psum | solution.py:182
  231.3 19.3 %all-to-all-start.6 = ((bf16[32,8,513]{2,1,0:T(8,128)(2,1)}), bf16[32,8,513]{2,1,0:T(8,128)(2,1)S(1)}, u32[]{:S(2)}, u32[]{:S(2)}) async-start(bf16[32,8,513]{2,1,0:T(8,128)(2,1)} %pad_maximum_fusion), calls=%async_computation.6 | async-start | bytes 655360 | tf_op jit(solution)/shard_map/all_to_all | solution.py:38
  252.5 10.9 %all-to-all-start.7 = ((bf16[32,2,256]{2,1,0:T(2,128)(2,1)}), bf16[32,2,256]{2,1,0:T(2,128)(2,1)S(1)}, u32[]{:S(2)}, u32[]{:S(2)}) async-start(bf16[32,2,256]{2,1,0:T(2,128)(2,1)} %reshape.477), calls=%async_computation.7 | async-start | bytes 65536 | tf_op jit(solution)/shard_map/all_to_all | solution.py:228
  256.1 87.8 %reduce-scatter.2.cloned.1.call-start = ((), (), s32[]{:S(2)}) async-start(), calls=%async_computation.11 | async-start | bytes 3276800 | tf_op jit(solution)/shard_map/reduce_scatter | solution.py:254
  272.6 10.5 %slice-start.4 = ((s8[7340032]{0:T(1024)(128)(4,1)}), s8[4194304]{0:T(1024)(128)(4,1)S(1)}, s32[]{:S(2)}) async-start(s8[7340032]{0:T(1024)(128)(4,1)} %bitcast.103), calls=%async_computation.16 | async-start | bytes 8388608
  272.9 10.2 %slice-start.5 = ((s8[7340032]{0:T(1024)(128)(4,1)}), s8[3145728]{0:T(1024)(128)(4,1)S(1)}, s32[]{:S(2)}) async-start(s8[7340032]{0:T(1024)(128)(4,1)} %bitcast.103), calls=%async_computation.17 | async-start | bytes 6291456
  357.3 26.7 %all-to-all-start.8 = ((bf16[32,2,8192]{2,1,0:T(2,128)(2,1)}), bf16[32,2,8192]{2,1,0:T(2,128)(2,1)}, u32[]{:S(2)}, u32[]{:S(2)}) async-start(bf16[32,2,8192]{2,1,0:T(2,128)(2,1)} %reshape.479), calls=%async_computation.9 | async-start | bytes 2097152 | tf_op jit(solution)/shard_map/all_to_all | solution.py:268
  (1 other events, 5.0 us)
Sparse Core Ops, SparseCore 0:
  190.1 36.8 all-reduce.3
  311.2 32.6 reduce-scatter.1
where the time goes:
time: 406 us; the launch traced here: 400 us
  waiting for transfers between devices  164 us (40%)
  matrix products  65.1 us (16%)
  blocking collectives  61 us (15%)
  starting transfers between devices  53.3 us (13%)
  local copies, waits for them, and re-layouts  26.3 us (6%)
  between operations  16.1 us (4%)
  other arithmetic  14.4 us (4%)
    dot_general x4, matrix products, contract_rows(): lax.dot_general(left, right, (((1,), (1,)), ((), ())), preferred_element_...  38.9 us
    psum x1, waiting for transfers between devices, per_device(): lax.psum(score_part.astype(jnp.bfloat16), 'mp').astype(jnp.float32)  37 us
    reduce_scatter x1, waiting for transfers between devices, per_device(): lax.psum_scatter(normed_grad.astype(jnp.bfloat16), 'mp', scatter_dimensio...  32.8 us
    all_to_all x1, waiting for transfers between devices, sent_to_all(): return lax.all_to_all(copies, axis, split_axis=0, concat_axis=0, tiled=True)  26.3 us
    all_gather x1, blocking collectives, per_device(): all_vec = lax.all_gather(passage_vec, 'dp', axis=0, tiled=True)  23.1 us
    all_to_all x1, waiting for transfers between devices, per_device(): lax.all_to_all(back.reshape(dp_count, slot_count, block_len * part_width)...  16.4 us
    all_to_all x1, waiting for transfers between devices, per_device(): lax.all_to_all(send, 'dp', split_axis=0, concat_axis=0, tiled=True)  15.6 us
    unnamed x1, blocking collectives  15.5 us
  transfers between devices with their start and end apart: 11, of which 11 were waited for; matrix products, arithmetic and copies ran while one was open for 3% of the time, Pallas kernels for 0%

commit v1 on v0

--- a/solution.py
+++ b/solution.py
@@ -10,6 +10,11 @@
 loss_seed = 4096.0
 norm_epsilon = 1e-05
 unit_epsilon = 1e-06
+
+
+def gather_from_all(x, axis, dim):
+    copies = jnp.concatenate([x] * lax.axis_size(axis), axis=dim)
+    return lax.all_to_all(copies, axis, dim, dim, tiled=True)
 
 
 def sent_to_all(x, axis):
@@ -170,7 +175,7 @@
     )
     divisor = jnp.maximum(token_total, 1.0)
     passage_vec = (passage_sum / divisor[:, None]).astype(jnp.bfloat16)
-    all_vec = lax.all_gather(passage_vec, "dp", axis=0, tiled=True)
+    all_vec = gather_from_all(passage_vec, "dp", 0)
     pass_total = all_vec.shape[0]
     all_live = (
         jnp.arange(pass_total, dtype=jnp.int32) % most_pass < jnp.repeat(all_counts, most_pass)

time: 406 us -> 414 us (1.020)
  blocking collectives: 61 us -> 37.9 us
  local copies, waits for them, and re-layouts: 26.3 us -> 44.9 us
  waiting for transfers between devices: 164 us -> 172 us
    all_gather x1 -> x0, blocking collectives: 23.1 us -> none  [per_device(): all_vec = lax.all_gather(passage_vec, 'dp', axis=0, tiled=True)]
    unnamed x40 -> x70, local copies, waits for them, and re-layouts: 14.7 us -> 32.7 us
    all_to_all x0 -> x1, waiting for transfers between devices: none -> 8.9 us  [gather_from_all(): return lax.all_to_all(copies, axis, dim, dim, tiled=True)]
  transfers between devices with their start and end apart: 11 -> 12, of which waited for: 11 -> 12; matrix products, arithmetic and copies ran while one was open for 3% -> 3% of each run, Pallas kernels for 0% -> 0%
where the time goes in v1:
time: 414 us; the launch traced here: 409 us
  waiting for transfers between devices  172 us (42%)
  matrix products  65.1 us (16%)
  starting transfers between devices  57.2 us (14%)
  local copies, waits for them, and re-layouts  44.9 us (11%)
  blocking collectives  37.9 us (9%)
  between operations  16.2 us (4%)
  other arithmetic  15 us (4%)
    dot_general x4, matrix products, contract_rows(): lax.dot_general(left, right, (((1,), (1,)), ((), ())), preferred_element_...  38.9 us
    psum x1, waiting for transfers between devices, per_device(): lax.psum(score_part.astype(jnp.bfloat16), 'mp').astype(jnp.float32)  36.1 us
    reduce_scatter x1, waiting for transfers between devices, per_device(): lax.psum_scatter(normed_grad.astype(jnp.bfloat16), 'mp', scatter_dimensio...  32.8 us
    unnamed x70, local copies, waits for them, and re-layouts  32.7 us
    all_to_all x1, waiting for transfers between devices, sent_to_all(): return lax.all_to_all(copies, axis, split_axis=0, concat_axis=0, tiled=True)  26.3 us
    all_to_all x1, waiting for transfers between devices, per_device(): lax.all_to_all(back.reshape(dp_count, slot_count, block_len * part_width)...  16.4 us
    all_to_all x1, waiting for transfers between devices, per_device(): lax.all_to_all(send, 'dp', split_axis=0, concat_axis=0, tiled=True)  15.6 us
    unnamed x1, blocking collectives  15.5 us
  transfers between devices with their start and end apart: 12, of which 12 were waited for; matrix products, arithmetic and copies ran while one was open for 3% of the time, Pallas kernels for 0%

profile of v1, /device:TPU:1, one launch (start us, length us, event | category | flops | bytes accessed | tf_op | source)
XLA Modules:
  0.0 408.6 jit_solution(4976151619109096763)
XLA Ops:
  11.0 15.5 %all-reduce = s32[64]{0:T(128)S(1)} all-reduce(s32[64]{0:T(128)S(1)} %dynamic-update-slice), channel_id=1, replica_groups=mesh['dp'=32,'mp'=4] {'dp'}, use_global_device_ids=true, to_apply=%add | all-reduce | flops 64 | bytes 512
  29.0 7.5 %all-to-all-start = ((bf16[32,1,1]{2,1,0:T(2,128)(2,1)}), bf16[32,1,1]{2,1,0:T(2,128)(2,1)S(1)}, u32[]{:S(2)}, u32[]{:S(2)}) async-start(bf16[32,1,1]{2,1,0:T(2,128)(2,1)} %copy.81), calls=%async_computation | async-start | bytes 32768 | tf_op jit(solution)/shard_map/all_to_all | solution.py:133
  49.2 15.6 %all-to-all-done.1 = bf16[32,1,32,512]{3,2,1,0:T(8,128)(2,1)S(1)} async-done(((bf16[32,1,32,512]{3,2,1,0:T(8,128)(2,1)}), bf16[32,1,32,512]{3,2,1,0:T(8,128)(2,1)S(1)}, u32[]{:S(2)}, u32[]{:S(2)}) %all-to-all-start.1) | async-done | bytes 1048608 | tf_op jit(solution)/shard_map/all_to_all | solution.py:131
  77.3 4.8 %all-to-all-start.3 = ((bf16[4,640,512]{1,2,0:T(8,128)(2,1)}), bf16[4,640,512]{1,2,0:T(8,128)(2,1)S(1)}, u32[]{:S(2)}, u32[]{:S(2)}) async-start(bf16[4,640,512]{1,2,0:T(8,128)(2,1)} %broadcast_in_dim.18), calls=%async_computation.3 | async-start | bytes 5242880 | tf_op jit(solution)/shard_map/all_to_all | solution.py:22
  86.4 26.3 %all-to-all-done.3 = bf16[4,640,512]{1,2,0:T(8,128)(2,1)S(1)} async-done(((bf16[4,640,512]{1,2,0:T(8,128)(2,1)}), bf16[4,640,512]{1,2,0:T(8,128)(2,1)S(1)}, u32[]{:S(2)}, u32[]{:S(2)}) %all-to-all-start.3) | async-done | bytes 2621472 | tf_op jit(solution)/shard_map/all_to_all | solution.py:22
  114.0 8.6 %fusion.86 = f32[640,1792]{1,0:T(8,128)S(1)} fusion(bf16[640,2048]{0,1:T(8,128)(2,1)S(1)} %fusion.2, bf16[2048,1792]{1,0:T(8,128)(2,1)} %param.16), kind=kOutput, calls=%fused_computation.205 | convolution fusion | flops 4697620480 | bytes 14548992 | tf_op jit(solution)/shard_map/dot_general | solution.py:149
  122.7 5.4 %fusion.85 = f32[640,1792]{1,0:T(8,128)S(1)} fusion(bf16[640,2048]{0,1:T(8,128)(2,1)S(1)} %fusion.2, bf16[2048,1792]{1,0:T(8,128)(2,1)S(1)} %bitcast.105), kind=kOutput, calls=%fused_computation.204 | convolution fusion | flops 4697620480 | bytes 14548992 | tf_op jit(solution)/shard_map/dot_general | solution.py:148
  128.2 5.0 %fusion.4 = f32[640,2048]{1,0:T(8,128)S(1)} fusion(bf16[1792,2048]{1,0:T(8,128)(2,1)S(1)} %bitcast.103, f32[640,1792]{1,0:T(8,128)S(1)} %fusion.86, f32[640,1792]{1,0:T(8,128)S(1)} %fusion.85), kind=kOutput, calls=%fused_computation.17 | convolution fusion | flops 4704501760 | bytes 21757952 | tf_op jit(solution)/shard_map/dot_general | solution.py:152
  144.8 6.5 %all-to-all-start.5 = ((bf16[32,2,256]{2,1,0:T(2,128)(2,1)}), bf16[32,2,256]{2,1,0:T(2,128)(2,1)S(1)}, u32[]{:S(2)}, u32[]{:S(2)}) async-start(bf16[32,2,256]{2,1,0:T(2,128)(2,1)} %reshape.479), calls=%async_computation.5 | async-start | bytes 65536 | tf_op jit(solution)/shard_map/all_to_all | solution.py:164
  151.4 7.3 %all-to-all-done.5 = bf16[32,2,256]{2,1,0:T(2,128)(2,1)S(1)} async-done(((bf16[32,2,256]{2,1,0:T(2,128)(2,1)}), bf16[32,2,256]{2,1,0:T(2,128)(2,1)S(1)}, u32[]{:S(2)}, u32[]{:S(2)}) %all-to-all-start.5) | async-done | bytes 32800 | tf_op jit(solution)/shard_map/all_to_all | solution.py:164
  182.3 8.9 %all-to-all-done.6 = bf16[32,8,512]{2,1,0:T(8,128)(2,1)S(1)} async-done(((bf16[32,8,512]{2,1,0:T(8,128)(2,1)}), bf16[32,8,512]{2,1,0:T(8,128)(2,1)S(1)}, u32[]{:S(2)}, u32[]{:S(2)}) %all-to-all-start.6) | async-done | bytes 262176 | tf_op jit(solution)/shard_map/all_to_all | solution.py:17
  191.4 6.9 %all-reduce.1 = (bf16[256]{0:T(256)(128)(2,1)S(1)}, bf16[128]{0:T(256)(128)(2,1)S(1)}) all-reduce(bf16[256]{0:T(256)(128)(2,1)S(1)} %convert_element_type.282, bf16[128]{0:T(256)(128)(2,1)S(1)} %multiply_reduce_fusion.3), channel_id=1, replica_groups=mesh['dp'=32,'mp'=4] {'mp'}, use_global_device_ids=true, to_apply=%region_15.16 | all-reduce | flops 384 | bytes 1536 | tf_op jit(solution)/shard_map/psum | solution.py:188
  199.2 36.1 %all-reduce.4.cloned.1.call-done = bf16[128,256]{0,1:T(8,128)(2,1)} async-done(((bf16[128,256]{0,1:T(8,128)(2,1)}), bf16[128,256]{0,1:T(8,128)(2,1)}) %all-reduce.4.cloned.1.call-update) | async-done | bytes 65552 | tf_op jit(solution)/shard_map/psum | solution.py:187
  239.6 9.7 %all-to-all-start.7 = ((bf16[32,8,513]{2,1,0:T(8,128)(2,1)}), bf16[32,8,513]{2,1,0:T(8,128)(2,1)S(1)}, u32[]{:S(2)}, u32[]{:S(2)}) async-start(bf16[32,8,513]{2,1,0:T(8,128)(2,1)} %pad_maximum_fusion), calls=%async_computation.7 | async-start | bytes 655360 | tf_op jit(solution)/shard_map/all_to_all | solution.py:43
  249.3 9.6 %all-to-all-done.7 = bf16[32,8,513]{2,1,0:T(8,128)(2,1)S(1)} async-done(((bf16[32,8,513]{2,1,0:T(8,128)(2,1)}), bf16[32,8,513]{2,1,0:T(8,128)(2,1)S(1)}, u32[]{:S(2)}, u32[]{:S(2)}) %all-to-all-start.7) | async-done | bytes 262688 | tf_op jit(solution)/shard_map/all_to_all | solution.py:43
  264.6 7.1 %all-to-all-done.8 = bf16[32,2,256]{2,1,0:T(2,128)(2,1)S(1)} async-done(((bf16[32,2,256]{2,1,0:T(2,128)(2,1)}), bf16[32,2,256]{2,1,0:T(2,128)(2,1)S(1)}, u32[]{:S(2)}, u32[]{:S(2)}) %all-to-all-start.8) | async-done | bytes 32800 | tf_op jit(solution)/shard_map/all_to_all | solution.py:233
  271.9 9.0 %all_gather.7 = bf16[20,2048]{1,0:T(8,128)(2,1)S(1)} all-gather(bf16[20,512]{1,0:T(8,128)(2,1)S(1)} %get-tuple-element.22), channel_id=1, replica_groups=mesh['dp'=32,'mp'=4] {'mp'}, dimensions={1}, use_global_device_ids=true | all-gather | bytes 102400 | tf_op jit(solution)/shard_map/all_gather | solution.py:243
  281.3 10.2 %fusion.87 = f32[640,1792]{1,0:T(8,128)} fusion(bf16[640,2048]{1,0:T(8,128)(2,1)S(1)} %fusion.3, bf16[1792,2048]{1,0:T(8,128)(2,1)} %param.17), kind=kOutput, calls=%fused_computation.206 | convolution fusion | flops 4697620480 | bytes 14548992 | tf_op jit(solution)/shard_map/dot_general | solution.py:60
  291.5 14.2 %fusion.7 = f32[640,2048]{1,0:T(8,128)} fusion(bf16[2048,1792]{1,0:T(8,128)(2,1)S(1)} %bitcast.107, f32[640,1792]{1,0:T(8,128)} %copy-done.6, f32[640,1792]{1,0:T(8,128)} %fusion.87, f32[640,1792]{1,0:T(8,128)} %copy-done.7), kind=kOutput, calls=%fused_computation.20 | convolution fusion | flops 4709089280 | bytes 26345472 | tf_op jit(solution)/shard_map/dot_general | solution.py:60
  305.7 13.7 %add_convert_fusion = bf16[640,2048]{1,0:T(8,128)(2,1)} fusion(f32[640,2048]{1,0:T(8,128)} %fusion.7, bf16[2048,1792]{1,0:T(8,128)(2,1)} %param.16, f32[640,1792]{1,0:T(8,128)} %fusion.87, f32[640,1792]{1,0:T(8,128)} %copy-done.6), kind=kOutput, calls=%fused_computation.10 | convolution fusion | flops 4707123200 | bytes 24379392 | tf_op jit(solution)/shard_map/dot_general | solution.py:60
  319.5 32.8 %reduce-scatter.2.cloned.1.call-done = bf16[640,512]{1,0:T(8,128)(2,1)} async-done(((bf16[640,2048]{1,0:T(8,128)(2,1)}), bf16[640,512]{1,0:T(8,128)(2,1)}) %reduce-scatter.2.cloned.1.call-update) | async-done | bytes 655376 | tf_op jit(solution)/shard_map/reduce_scatter | solution.py:259
  353.7 6.5 %psum.31 = f32[640]{0:T(1024)S(1)} all-reduce(f32[640]{0:T(1024)S(1)} %fusion.11), channel_id=1, replica_groups=mesh['dp'=32,'mp'=4] {'mp'}, use_global_device_ids=true, to_apply=%region_23.24 | all-reduce | flops 640 | bytes 5120 | tf_op jit(solution)/shard_map/psum | solution.py:263
  365.7 9.7 %all-to-all-start.9 = ((bf16[32,2,8192]{2,1,0:T(2,128)(2,1)}), bf16[32,2,8192]{2,1,0:T(2,128)(2,1)}, u32[]{:S(2)}, u32[]{:S(2)}) async-start(bf16[32,2,8192]{2,1,0:T(2,128)(2,1)} %reshape.483), calls=%async_computation.10 | async-start | bytes 2097152 | tf_op jit(solution)/shard_map/all_to_all | solution.py:273
  375.9 16.4 %all-to-all-done.9 = bf16[32,2,8192]{2,1,0:T(2,128)(2,1)} async-done(((bf16[32,2,8192]{2,1,0:T(2,128)(2,1)}), bf16[32,2,8192]{2,1,0:T(2,128)(2,1)}, u32[]{:S(2)}, u32[]{:S(2)}) %all-to-all-start.9) | async-done | bytes 1048608 | tf_op jit(solution)/shard_map/all_to_all | solution.py:273
  (178 shorter events, 99.1 us)
Async XLA Ops:
  7.2 40.6 %copy-start.3 = (s32[1024]{0:T(1024)S(1)}, s32[1024]{0:T(1024)}, u32[]{:S(2)}) copy-start(s32[1024]{0:T(1024)} %param.10) | copy-start | bytes 12292
  29.0 14.5 %all-to-all-start = ((bf16[32,1,1]{2,1,0:T(2,128)(2,1)}), bf16[32,1,1]{2,1,0:T(2,128)(2,1)S(1)}, u32[]{:S(2)}, u32[]{:S(2)}) async-start(bf16[32,1,1]{2,1,0:T(2,128)(2,1)} %copy.81), calls=%async_computation | async-start | bytes 32768 | tf_op jit(solution)/shard_map/all_to_all | solution.py:133
  43.5 21.2 %all-to-all-start.1 = ((bf16[32,1,32,512]{3,2,1,0:T(8,128)(2,1)}), bf16[32,1,32,512]{3,2,1,0:T(8,128)(2,1)S(1)}, u32[]{:S(2)}, u32[]{:S(2)}) async-start(bf16[32,1,32,512]{3,2,1,0:T(8,128)(2,1)} %bitcast.5), calls=%async_computation.1 | async-start | bytes 2097152 | tf_op jit(solution)/shard_map/all_to_all | solution.py:131
  64.7 10.9 %all-to-all-start.2 = ((bf16[32,1,32]{2,1,0:T(2,128)(2,1)}), bf16[32,1,32]{2,1,0:T(2,128)(2,1)S(1)}, u32[]{:S(2)}, u32[]{:S(2)}) async-start(bf16[32,1,32]{2,1,0:T(2,128)(2,1)} %copy.84), calls=%async_computation.2 | async-start | bytes 32768 | tf_op jit(solution)/shard_map/all_to_all | solution.py:132
  71.6 10.6 %copy-start.5 = (s32[2]{0:T(128)S(1)}, s32[2]{0:T(128)}, u32[]{:S(2)}) copy-start(s32[2]{0:T(128)} %param.11) | copy-start | bytes 28
  77.3 36.0 %copy-start.2 = (f32[2048]{0:T(1024)S(1)}, f32[2048]{0:T(1024)}, u32[]{:S(2)}) copy-start(f32[2048]{0:T(1024)} %param.14) | copy-start | bytes 24580
  77.3 35.4 %all-to-all-start.3 = ((bf16[4,640,512]{1,2,0:T(8,128)(2,1)}), bf16[4,640,512]{1,2,0:T(8,128)(2,1)S(1)}, u32[]{:S(2)}, u32[]{:S(2)}) async-start(bf16[4,640,512]{1,2,0:T(8,128)(2,1)} %broadcast_in_dim.18), calls=%async_computation.3 | async-start | bytes 5242880 | tf_op jit(solution)/shard_map/all_to_all | solution.py:22
  113.3 9.3 %slice-start.2 = ((s8[7340032]{0:T(1024)(128)(4,1)}), s8[4194304]{0:T(1024)(128)(4,1)S(1)}, s32[]{:S(2)}) async-start(s8[7340032]{0:T(1024)(128)(4,1)} %bitcast.104), calls=%async_computation.15 | async-start | bytes 8388608
  114.0 8.7 %slice-start.3 = ((s8[7340032]{0:T(1024)(128)(4,1)}), s8[3145728]{0:T(1024)(128)(4,1)S(1)}, s32[]{:S(2)}) async-start(s8[7340032]{0:T(1024)(128)(4,1)} %bitcast.104), calls=%async_computation.16 | async-start | bytes 6291456
  114.0 14.2 %slice-start = ((s8[7340032]{0:T(1024)(128)(4,1)}), s8[4194304]{0:T(1024)(128)(4,1)S(1)}, s32[]{:S(2)}) async-start(s8[7340032]{0:T(1024)(128)(4,1)} %bitcast.102), calls=%async_computation.13 | async-start | bytes 8388608
  122.7 5.5 %copy-start.7 = (f32[640,1792]{1,0:T(8,128)}, f32[640,1792]{1,0:T(8,128)S(1)}, u32[]{:S(2)}) copy-start(f32[640,1792]{1,0:T(8,128)S(1)} %fusion.86) | copy-start | bytes 13762564
  122.7 5.5 %slice-start.1 = ((s8[7340032]{0:T(1024)(128)(4,1)}), s8[3145728]{0:T(1024)(128)(4,1)S(1)}, s32[]{:S(2)}) async-start(s8[7340032]{0:T(1024)(128)(4,1)} %bitcast.102), calls=%async_computation.14 | async-start | bytes 6291456
  133.2 48.9 %copy-start.1 = (bf16[128,512]{1,0:T(8,128)(2,1)S(1)}, bf16[128,512]{1,0:T(8,128)(2,1)}, u32[]{:S(2)}) copy-start(bf16[128,512]{1,0:T(8,128)(2,1)} %param.13) | copy-start | bytes 393220
  133.2 49.0 %copy-start.4 = (s32[128]{0:T(128)S(1)}, s32[128]{0:T(128)}, u32[]{:S(2)}) copy-start(s32[128]{0:T(128)} %param.12) | copy-start | bytes 1540
  134.9 7.9 %all-to-all-start.4 = ((bf16[4,20,512]{2,1,0:T(8,128)(2,1)}), bf16[4,20,512]{2,1,0:T(8,128)(2,1)S(1)}, u32[]{:S(2)}, u32[]{:S(2)}) async-start(bf16[4,20,512]{2,1,0:T(8,128)(2,1)} %copy.86), calls=%async_computation.4 | async-start | bytes 196608 | tf_op jit(solution)/shard_map/all_to_all | solution.py:43
  144.8 13.9 %all-to-all-start.5 = ((bf16[32,2,256]{2,1,0:T(2,128)(2,1)}), bf16[32,2,256]{2,1,0:T(2,128)(2,1)S(1)}, u32[]{:S(2)}, u32[]{:S(2)}) async-start(bf16[32,2,256]{2,1,0:T(2,128)(2,1)} %reshape.479), calls=%async_computation.5 | async-start | bytes 65536 | tf_op jit(solution)/shard_map/all_to_all | solution.py:164
  178.1 13.0 %all-to-all-start.6 = ((bf16[32,8,512]{2,1,0:T(8,128)(2,1)}), bf16[32,8,512]{2,1,0:T(8,128)(2,1)S(1)}, u32[]{:S(2)}, u32[]{:S(2)}) async-start(bf16[32,8,512]{2,1,0:T(8,128)(2,1)} %bitcast.12), calls=%async_computation.6 | async-start | bytes 524288 | tf_op jit(solution)/shard_map/all_to_all | solution.py:17
  182.1 53.2 %all-reduce.4.cloned.1.call-start = ((), (), s32[]{:S(2)}) async-start(), calls=%async_computation.11 | async-start | bytes 131072 | tf_op jit(solution)/shard_map/psum | solution.py:187
  239.6 19.3 %all-to-all-start.7 = ((bf16[32,8,513]{2,1,0:T(8,128)(2,1)}), bf16[32,8,513]{2,1,0:T(8,128)(2,1)S(1)}, u32[]{:S(2)}, u32[]{:S(2)}) async-start(bf16[32,8,513]{2,1,0:T(8,128)(2,1)} %pad_maximum_fusion), calls=%async_computation.7 | async-start | bytes 655360 | tf_op jit(solution)/shard_map/all_to_all | solution.py:43
  260.8 10.9 %all-to-all-start.8 = ((bf16[32,2,256]{2,1,0:T(2,128)(2,1)}), bf16[32,2,256]{2,1,0:T(2,128)(2,1)S(1)}, u32[]{:S(2)}, u32[]{:S(2)}) async-start(bf16[32,2,256]{2,1,0:T(2,128)(2,1)} %reshape.481), calls=%async_computation.8 | async-start | bytes 65536 | tf_op jit(solution)/shard_map/all_to_all | solution.py:233
  264.5 87.8 %reduce-scatter.2.cloned.1.call-start = ((), (), s32[]{:S(2)}) async-start(), calls=%async_computation.12 | async-start | bytes 3276800 | tf_op jit(solution)/shard_map/reduce_scatter | solution.py:259
  280.9 10.5 %slice-start.4 = ((s8[7340032]{0:T(1024)(128)(4,1)}), s8[4194304]{0:T(1024)(128)(4,1)S(1)}, s32[]{:S(2)}) async-start(s8[7340032]{0:T(1024)(128)(4,1)} %bitcast.106), calls=%async_computation.17 | async-start | bytes 8388608
  281.3 10.2 %slice-start.5 = ((s8[7340032]{0:T(1024)(128)(4,1)}), s8[3145728]{0:T(1024)(128)(4,1)S(1)}, s32[]{:S(2)}) async-start(s8[7340032]{0:T(1024)(128)(4,1)} %bitcast.106), calls=%async_computation.18 | async-start | bytes 6291456
  365.7 26.7 %all-to-all-start.9 = ((bf16[32,2,8192]{2,1,0:T(2,128)(2,1)}), bf16[32,2,8192]{2,1,0:T(2,128)(2,1)}, u32[]{:S(2)}, u32[]{:S(2)}) async-start(bf16[32,2,8192]{2,1,0:T(2,128)(2,1)} %reshape.483), calls=%async_computation.10 | async-start | bytes 2097152 | tf_op jit(solution)/shard_map/all_to_all | solution.py:273
  (2 other events, 10.0 us)
Sparse Core Ops, SparseCore 0:
  199.3 35.9 all-reduce.3
  319.5 32.7 reduce-scatter.1
